TPU v7x, 32 devices: a whole 2x2x4 slice. The times are simulated.
32 devices in a mesh: tm: 16 (over z, y, x), space: 2 (over core).
Axes of the slice: x: 2, y: 2, z: 4, core: 2. Of those that a mesh axis runs over, the one named last changes fastest.
Arguments:
- features: bfloat16 [16, 16, 16, 256], P('tm', 'space'), may hold values from -6 to 6
- masks: int32 [16, 16, 16], P('tm', 'space'), may hold values from 0 to 1
- w_pix: bfloat16 [256, 256], replicated, may hold values from -0.375 to 0.375
- mask_embed: bfloat16 [256], replicated, may hold values from -4 to 4
- w_conv: bfloat16 [3, 3, 256, 256], replicated, may hold values from -0.125 to 0.125
- w_out: bfloat16 [256, 64], replicated, may hold values from -0.375 to 0.375
- w_ptr: bfloat16 [256, 256], replicated, may hold values from -0.375 to 0.375
- w_query: bfloat16 [256, 256], replicated, may hold values from -1 to 1
- w_key: bfloat16 [64, 256], replicated, may hold values from -0.75 to 0.75
- w_value: bfloat16 [64, 256], replicated, may hold values from -0.75 to 0.75
- w_proj: bfloat16 [256, 256], replicated, may hold values from -0.375 to 0.375
- mem_tpos: bfloat16 [3, 64], replicated, may hold values from -120 to 120
- ptr_tpos: bfloat16 [16, 256], replicated, may hold values from -4 to 4
- empty_memory: bfloat16 [64], replicated, may hold values from -4 to 4
Outputs:
- attended: bfloat16 [16, 16, 16, 256], P('tm', 'space')
- memory: bfloat16 [16, 16, 1024], P('tm', 'space')
- pointers: bfloat16 [16, 256], P('tm')
All inputs are finite; a program needn't handle non-finite values.
Results may differ from a plain program's by a relative error of at most 0.015.
The roundings to bfloat16 on the way count: a program that leaves them out, or rounds other values in their place, can miss the bound.
Values may be sent and summed in bfloat16 or wider, within the bound.
A program may use at most 128 MiB of HBM per device.

v0:
```python
import jax
import jax.numpy as jnp
from jax import lax
from jax.sharding import PartitionSpec as P

MEMS = 3
POINTERS = 16


def from_behind(block, axis, distance):
    devices = range(lax.axis_size(axis))
    route = [(i - distance, i) for i in devices if i - distance in devices]
    return lax.ppermute(block, axis, route)


def with_halo(block, sides, width):
    for axis, dim in sides:
        count = lax.axis_size(axis)
        forward = [(i, i + 1) for i in range(count - 1)]
        backward = [(target, source) for source, target in forward]
        low = lax.ppermute(
            lax.slice_in_dim(block, block.shape[dim] - width, None, axis=dim), axis, forward
        )
        high = lax.ppermute(lax.slice_in_dim(block, 0, width, axis=dim), axis, backward)
        block = jnp.concatenate([low, block, high], axis=dim)
    return block


def fetch_earlier(carried, hop_count):
    pieces = []
    for step_index in range(hop_count):
        pieces.append(from_behind(carried, "tm", step_index + 1))
    return jnp.concatenate(pieces[::-1], axis=0)


def attend(query, blocks):
    scores = []
    row_top = None
    for key_rows, value_rows, is_valid in blocks:
        block_scores = lax.dot_general(
            query, key_rows, (((1,), (1,)), ((), ())), preferred_element_type=jnp.float32
        )
        block_scores = jnp.where(is_valid, block_scores, -jnp.inf)
        scores.append(block_scores)
        block_top = jnp.max(block_scores, axis=1, keepdims=True)
        row_top = block_top if row_top is None else jnp.maximum(row_top, block_top)
    row_total = jnp.zeros_like(row_top)
    for block_scores in scores:
        row_total = row_total + jnp.sum(jnp.exp(block_scores - row_top), axis=1, keepdims=True)
    mixed_sum = jnp.zeros((query.shape[0], blocks[0][1].shape[1]), jnp.float32)
    for block_scores, block in zip(scores, blocks):
        weights = (jnp.exp(block_scores - row_top) / row_total).astype(jnp.bfloat16)
        mixed_sum = mixed_sum + jnp.dot(weights, block[1], preferred_element_type=jnp.float32)
    return mixed_sum.astype(jnp.bfloat16)


def body(
    features,
    masks,
    w_pix,
    mask_embed,
    w_conv,
    w_out,
    w_ptr,
    w_query,
    w_key,
    w_value,
    w_proj,
    mem_tpos,
    ptr_tpos,
    empty_memory,
):
    frames_dev, rows_dev, columns, model_dim = features.shape
    mem_dim = w_key.shape[0]
    ptr_tok = model_dim // mem_dim
    band_tokens = rows_dev * columns
    flat_rows = features.reshape(frames_dev * band_tokens, model_dim)
    mask_rows = masks.reshape(frames_dev * band_tokens, 1).astype(jnp.float32)
    joined_map = (
        jnp.dot(flat_rows, w_pix, preferred_element_type=jnp.float32)
        + mask_rows * mask_embed.astype(jnp.float32)
    ).astype(jnp.bfloat16)
    joined_map = joined_map.reshape(frames_dev, rows_dev, columns, model_dim)
    padded = with_halo(joined_map, (("space", 1),), 1)
    padded = jnp.pad(padded, ((0, 0), (0, 0), (1, 1), (0, 0)))
    conv_sum = jnp.zeros((frames_dev * band_tokens, model_dim), jnp.float32)
    for row_tap in range(3):
        for col_tap in range(3):
            window_rows = padded[
                :, row_tap : row_tap + rows_dev, col_tap : col_tap + columns, :
            ].reshape(-1, model_dim)
            conv_sum = conv_sum + jnp.dot(
                window_rows, w_conv[row_tap, col_tap], preferred_element_type=jnp.float32
            )
    hidden = jax.nn.gelu(conv_sum, approximate=True).astype(jnp.bfloat16)
    memory = jnp.dot(hidden, w_out, preferred_element_type=jnp.float32).astype(jnp.bfloat16)
    memory = memory.reshape(frames_dev, rows_dev, columns * mem_dim)
    band_mask = masks.reshape(frames_dev, band_tokens).astype(jnp.bfloat16)
    partial_value = jnp.einsum(
        "ft,ftd->fd",
        band_mask,
        features.reshape(frames_dev, band_tokens, model_dim),
        preferred_element_type=jnp.float32,
    )
    pooled = lax.psum(partial_value, "space")
    normed = (pooled * lax.rsqrt(jnp.mean(pooled * pooled, axis=1, keepdims=True) + 1e-06)).astype(
        jnp.bfloat16
    )
    pointers = jnp.dot(normed, w_ptr, preferred_element_type=jnp.float32).astype(jnp.bfloat16)
    all_pointers = lax.all_gather(pointers, "tm", axis=0, tiled=True)
    hop_count = (MEMS + frames_dev - 1) // frames_dev
    carried = lax.all_gather(memory, "space", axis=1, tiled=True)
    history = jnp.concatenate(
        [fetch_earlier(carried, hop_count), carried[: frames_dev - 1]], axis=0
    )
    grid_tokens = columns * columns
    hist_frames = history.shape[0]
    history = history.reshape(hist_frames, grid_tokens, mem_dim)
    hist_values = jnp.dot(
        history.reshape(-1, mem_dim), w_value, preferred_element_type=jnp.float32
    ).astype(jnp.bfloat16)
    hist_values = hist_values.reshape(hist_frames, grid_tokens, model_dim)
    tpos_keys = jnp.dot(mem_tpos, w_key, preferred_element_type=jnp.float32)
    ptr_tpos_keys = jnp.dot(
        ptr_tpos[::-1].reshape(POINTERS * ptr_tok, mem_dim),
        w_key,
        preferred_element_type=jnp.float32,
    )
    null_key = jnp.dot(
        empty_memory.reshape(1, mem_dim), w_key, preferred_element_type=jnp.float32
    ).astype(jnp.bfloat16)
    null_value = jnp.dot(
        empty_memory.reshape(1, mem_dim), w_value, preferred_element_type=jnp.float32
    ).astype(jnp.bfloat16)
    padded_ptr = jnp.concatenate(
        [jnp.zeros((POINTERS, model_dim), jnp.bfloat16), all_pointers], axis=0
    )
    ptr_offsets = jnp.repeat(jnp.arange(POINTERS, dtype=jnp.int32) - POINTERS, ptr_tok)
    features_f = features.reshape(frames_dev, band_tokens, model_dim).astype(jnp.float32)
    first_frame = lax.axis_index("tm") * frames_dev
    frame = first_frame + 0
    rows_f = features_f[0]
    centred = rows_f - jnp.mean(rows_f, axis=1, keepdims=True)
    query_in = (
        centred * lax.rsqrt(jnp.mean(centred * centred, axis=1, keepdims=True) + 1e-05)
    ).astype(jnp.bfloat16)
    query = (
        jnp.dot(query_in, w_query, preferred_element_type=jnp.float32) * model_dim ** (-0.5)
    ).astype(jnp.bfloat16)
    blocks = []
    for distance in range(1, MEMS + 1):
        slot_index = hop_count * frames_dev - distance
        key_rows = (
            jnp.dot(history[slot_index], w_key, preferred_element_type=jnp.float32)
            + tpos_keys[distance - 1]
        ).astype(jnp.bfloat16)
        blocks.append((key_rows, hist_values[slot_index], frame - distance >= 0))
    window = lax.dynamic_slice_in_dim(padded_ptr, frame, POINTERS, 0)
    ptr_tokens = window.reshape(POINTERS * ptr_tok, mem_dim)
    ptr_keys = (
        jnp.dot(ptr_tokens, w_key, preferred_element_type=jnp.float32) + ptr_tpos_keys
    ).astype(jnp.bfloat16)
    ptr_values = jnp.dot(ptr_tokens, w_value, preferred_element_type=jnp.float32).astype(
        jnp.bfloat16
    )
    extra_valid = jnp.concatenate([frame + ptr_offsets >= 0, jnp.ones((1,), bool)], axis=0)
    blocks.append(
        (
            jnp.concatenate([ptr_keys, null_key], axis=0),
            jnp.concatenate([ptr_values, null_value], axis=0),
            extra_valid[None, :],
        )
    )
    mixed_rows = attend(query, blocks)
    outputs = [
        (rows_f + jnp.dot(mixed_rows, w_proj, preferred_element_type=jnp.float32)).astype(
            jnp.bfloat16
        )
    ]
    attended = jnp.stack(outputs, axis=0).reshape(frames_dev, rows_dev, columns, model_dim)
    return (attended, memory, pointers)


def solution(mesh):
    return jax.shard_map(
        body,
        mesh=mesh,
        in_specs=(
            P("tm", "space", None, None),
            P("tm", "space", None),
            P(),
            P(),
            P(),
            P(),
            P(),
            P(),
            P(),
            P(),
            P(),
            P(),
            P(),
            P(),
        ),
        out_specs=(P("tm", "space", None, None), P("tm", "space", None), P("tm", None)),
        check_vma=False,
    )
```

profile of v0, /device:TPU:24, one launch (start us, length us, event | category | flops | bytes accessed | tf_op | source)
XLA Modules:
  0.0 78.9 jit_solution(8171158523613113094)
XLA Ops:
  0.7 0.7 convert_element_type.111
  1.4 0.8 convert_bitcast_fusion
  2.3 1.0 %fusion.12 = bf16[128,256]{1,0:T(8,128)(2,1)S(1)} fusion(bf16[128,256]{1,0:T(8,128)(2,1)} %bitcast.107, bf16[256,256]{1,0:T(8,128)(2,1)S(1)} %copy-done, f32[256]{0:T(256)S(1)} %convert_element_type.111, f32[128]{0:T(128)S(1)} %convert_element_type.110), kind=kOutput, calls=%fused_computation.29 | convolution fusion | flops 16875520 | bytes 263680 | tf_op jit(solution)/shard_map/dot_general | solution.py:80
  3.3 1.3 %collective-permute-start.1 = (bf16[1,1,16,256]{3,2,1,0:T(8,128)(2,1)S(1)}, bf16[1,1,16,256]{3,2,1,0:T(8,128)(2,1)S(1)}, u32[]{:S(2)}, u32[]{:S(2)}) collective-permute-start(bf16[1,1,16,256]{3,2,1,0:T(8,128)(2,1)S(1)} %get-tuple-element.15), channel_id=1, source_target_pairs={{1,0},{3,2},{5,4},{7,6},{9,8},{11,10},{13,12},{15,14},{17,16},{19,... | collective-permute-start | bytes 24584 | tf_op jit(solution)/shard_map/ppermute | solution.py:24
  4.6 3.0 %collective-permute-start = (bf16[1,1,16,256]{3,2,1,0:T(8,128)(2,1)S(1)}, bf16[1,1,16,256]{3,2,1,0:T(8,128)(2,1)S(1)}, u32[]{:S(2)}, u32[]{:S(2)}) collective-permute-start(bf16[1,1,16,256]{3,2,1,0:T(8,128)(2,1)S(1)} %get-tuple-element.14), channel_id=1, source_target_pairs={{0,1},{2,3},{4,5},{6,7},{8,9},{10,11},{12,13},{14,15},{16,17},{18,... | collective-permute-start | bytes 24584 | tf_op jit(solution)/shard_map/ppermute | solution.py:21
  7.6 0.9 %convert_reduce_fusion = f32[8,16]{1,0:T(8,128)S(1)} fusion(bf16[1,8,16,256]{3,2,1,0:T(8,128)(2,1)} %param.14), kind=kLoop, calls=%fused_computation.42 | loop fusion | flops 65408 | bytes 66048 | tf_op jit(solution)/shard_map/reduce_sum | solution.py:143
  8.6 1.1 %fusion.22 = f32[8,16]{1,0:T(8,128)S(1)} fusion(bf16[1,8,16,256]{3,2,1,0:T(8,128)(2,1)} %param.14, f32[8,16]{1,0:T(8,128)S(1)} %broadcast_multiply_fusion), kind=kLoop, calls=%fused_computation.50 | loop fusion | flops 130944 | bytes 66560 | tf_op jit(solution)/shard_map/reduce_sum | solution.py:145
  9.8 0.9 %fusion.117 = f32[3,256]{1,0:T(4,128)S(1)} fusion(bf16[3,64]{1,0:T(4,128)(2,1)} %param.25, bf16[64,256]{1,0:T(8,128)(2,1)} %param.22), kind=kOutput, calls=%fused_computation.157 | convolution fusion | flops 98304 | bytes 36224 | tf_op jit(solution)/shard_map/dot_general | solution.py:123
  10.8 0.9 %fusion.100 = f32[1,256]{1,0:T(1,128)S(1)} fusion(bf16[64,256]{1,0:T(8,128)(2,1)} %param.22, bf16[64]{0:T(256)(128)(2,1)} %param.27), kind=kOutput, calls=%fused_computation.138 | convolution fusion | flops 32768 | bytes 33920 | tf_op jit(solution)/shard_map/dot_general | solution.py:129
  11.7 1.0 %convolution_bitcast_fusion = f32[1,256]{1,0:T(1,128)S(1)} fusion(bf16[1,8,16,256]{3,2,1,0:T(8,128)(2,1)} %param.14, bf16[8,16,1]{1,0,2:T(8,128)(2,1)S(1)} %get-tuple-element.19), kind=kOutput, calls=%fused_computation.36 | convolution fusion | flops 65536 | bytes 66816 | tf_op jit(solution)/shard_map/ft,ftd->fd/dot_general | solution.py:99
  12.7 2.4 %psum.7 = f32[1,256]{1,0:T(1,128)S(1)} all-reduce(f32[1,256]{1,0:T(1,128)S(1)} %convolution_bitcast_fusion), channel_id=1, replica_groups=mesh['tm'=16,'space'=2] {'space'}, use_global_device_ids=true, to_apply=%region_5.6 | all-reduce | flops 256 | bytes 2048 | tf_op jit(solution)/shard_map/psum | solution.py:105
  15.2 0.6 multiply_reduce_fusion
  16.5 1.0 %fusion.94 = f32[1,256]{1,0:T(1,128)S(1)} fusion(bf16[256,256]{1,0:T(8,128)(2,1)} %param.20, f32[1,256]{1,0:T(1,128)S(1)} %psum.7, f32[]{:T(128)S(6)} %rsqrt.17), kind=kOutput, calls=%fused_computation.131 | convolution fusion | flops 131584 | bytes 133124 | tf_op jit(solution)/shard_map/dot_general | solution.py:109
  17.5 32.6 %all-gather.1 = bf16[16,1,256]{2,1,0:T(2,128)(2,1)S(1)} all-gather(bf16[1,1,256]{2,1,0:T(2,128)(2,1)S(1)} %reshape.203), channel_id=2, replica_groups=mesh['tm'=16,'space'=2] {'tm'}, dimensions={0}, use_global_device_ids=true | all-gather | bytes 8704 | tf_op jit(solution)/shard_map/all_gather | solution.py:110
  50.2 0.9 %fusion.118 = f32[64,256]{1,0:T(8,128)S(1)} fusion(bf16[64,64]{1,0:T(8,128)(2,1)S(1)} %reshape.200, bf16[64,256]{1,0:T(8,128)(2,1)} %param.22), kind=kOutput, calls=%fused_computation.158 | convolution fusion | flops 2097152 | bytes 106496 | tf_op jit(solution)/shard_map/dot_general | solution.py:161
  51.1 0.7 rev.3
  52.1 0.9 %convolution_convert_fusion.1 = bf16[64,256]{1,0:T(8,128)(2,1)S(1)} fusion(bf16[64,64]{1,0:T(8,128)(2,1)S(1)} %reshape.200, bf16[64,256]{1,0:T(8,128)(2,1)} %param.23), kind=kOutput, calls=%fused_computation.33 | convolution fusion | flops 2113536 | bytes 73728 | tf_op jit(solution)/shard_map/dot_general | solution.py:163
  53.0 0.9 %fusion.14 = bf16[64,256]{1,0:T(8,128)(2,1)S(1)} fusion(f32[64,256]{1,0:T(8,128)S(1)} %fusion.118, bf16[64,64]{1,0:T(8,128)(2,1)S(1)} %reshape.201, bf16[64,256]{1,0:T(8,128)(2,1)} %param.22), kind=kOutput, calls=%fused_computation.32 | convolution fusion | flops 2129920 | bytes 139264 | tf_op jit(solution)/shard_map/dot_general | solution.py:124
  56.6 1.8 %all_gather.6 = bf16[1,16,1024]{2,1,0:T(8,128)(2,1)S(1)} all-gather(bf16[1,8,1024]{2,1,0:T(8,128)(2,1)S(1)} %reshape.196), channel_id=1, replica_groups=mesh['tm'=16,'space'=2] {'space'}, dimensions={1}, use_global_device_ids=true | all-gather | bytes 49152 | tf_op jit(solution)/shard_map/all_gather | solution.py:112
  58.4 3.4 %collective-permute-start.2 = (bf16[1,16,1024]{2,1,0:T(8,128)(2,1)S(1)}, bf16[1,16,1024]{2,1,0:T(8,128)(2,1)S(1)}, u32[]{:S(2)}, u32[]{:S(2)}) collective-permute-start(bf16[1,16,1024]{2,1,0:T(8,128)(2,1)S(1)} %all_gather.6), channel_id=1, source_target_pairs={{0,2},{2,4},{4,6},{6,8},{8,10},{10,12},{12,14},{14,16},{16,18},{18... | collective-permute-start | bytes 98312 | tf_op jit(solution)/shard_map/ppermute | solution.py:13
  61.9 6.1 %collective-permute-start.3 = (bf16[1,16,1024]{2,1,0:T(8,128)(2,1)S(1)}, bf16[1,16,1024]{2,1,0:T(8,128)(2,1)S(1)}, u32[]{:S(2)}, u32[]{:S(2)}) collective-permute-start(bf16[1,16,1024]{2,1,0:T(8,128)(2,1)S(1)} %all_gather.6), channel_id=1, source_target_pairs={{0,4},{2,6},{4,8},{6,10},{8,12},{10,14},{12,16},{14,18},{16,20},{1... | collective-permute-start | bytes 98312 | tf_op jit(solution)/shard_map/ppermute | solution.py:13
  68.0 1.9 %collective-permute-start.4 = (bf16[1,16,1024]{2,1,0:T(8,128)(2,1)S(1)}, bf16[1,16,1024]{2,1,0:T(8,128)(2,1)S(1)}, u32[]{:S(2)}, u32[]{:S(2)}) collective-permute-start(bf16[1,16,1024]{2,1,0:T(8,128)(2,1)S(1)} %all_gather.6), channel_id=1, source_target_pairs={{0,6},{2,8},{4,10},{6,12},{8,14},{10,16},{12,18},{14,20},{16,22},{... | collective-permute-start | bytes 98312 | tf_op jit(solution)/shard_map/ppermute | solution.py:13
  70.5 4.2 %collective-permute-done.4 = bf16[1,16,1024]{2,1,0:T(8,128)(2,1)S(1)} collective-permute-done((bf16[1,16,1024]{2,1,0:T(8,128)(2,1)S(1)}, bf16[1,16,1024]{2,1,0:T(8,128)(2,1)S(1)}, u32[]{:S(2)}, u32[]{:S(2)}) %collective-permute-start.4) | collective-permute-done | bytes 32800 | tf_op jit(solution)/shard_map/ppermute | solution.py:13
  78.0 1.0 %fusion.13 = bf16[128,256]{1,0:T(8,128)(2,1)} fusion(bf16[256,256]{1,0:T(8,128)(2,1)S(1)} %copy-done.5, f32[128,256]{1,0:T(8,128)S(1)} %convolution_add_fusion.5, bf16[128,256]{1,0:T(8,128)(2,1)S(1)} %bitcast.109, bf16[1,256]{1,0:T(2,128)(2,1)S(1)} %convert_element_type.132, bf16[64,256]{1,0:T(8,128)(2,1)S(1)} %convolution_convert_fusion.1, ...), kind=kOutput, calls=%fused_computation.30 | convolution fusion | flops 21292416 | bytes 460800 | tf_op jit(solution)/shard_map/dot_general | solution.py:176
  (79 shorter events, 7.1 us)
Async XLA Ops:
  0.6 1.6 %copy-start = (bf16[256,256]{1,0:T(8,128)(2,1)S(1)}, bf16[256,256]{1,0:T(8,128)(2,1)}, u32[]{:S(2)}) copy-start(bf16[256,256]{1,0:T(8,128)(2,1)} %param.16) | copy-start | bytes 393220
  0.6 53.3 %copy-start.2 = (bf16[1,8,16,256]{3,2,1,0:T(8,128)(2,1)S(1)}, bf16[1,8,16,256]{3,2,1,0:T(8,128)(2,1)}, u32[]{:S(2)}) copy-start(bf16[1,8,16,256]{3,2,1,0:T(8,128)(2,1)} %param.14) | copy-start | bytes 196612
  0.7 53.7 %copy-start.7 = (bf16[64]{0:T(256)(128)(2,1)S(1)}, bf16[64]{0:T(256)(128)(2,1)}, u32[]{:S(2)}) copy-start(bf16[64]{0:T(256)(128)(2,1)} %param.27) | copy-start | bytes 388
  0.7 53.7 %copy-start.4 = (bf16[64,256]{1,0:T(8,128)(2,1)S(1)}, bf16[64,256]{1,0:T(8,128)(2,1)}, u32[]{:S(2)}) copy-start(bf16[64,256]{1,0:T(8,128)(2,1)} %param.23) | copy-start | bytes 98308
  0.7 53.3 %copy-start.8 = (bf16[256,256]{1,0:T(8,128)(2,1)S(1)}, bf16[256,256]{1,0:T(8,128)(2,1)}, u32[]{:S(2)}) copy-start(bf16[256,256]{1,0:T(8,128)(2,1)} %param.21) | copy-start | bytes 393220
  3.3 51.2 %collective-permute-start.1 = (bf16[1,1,16,256]{3,2,1,0:T(8,128)(2,1)S(1)}, bf16[1,1,16,256]{3,2,1,0:T(8,128)(2,1)S(1)}, u32[]{:S(2)}, u32[]{:S(2)}) collective-permute-start(bf16[1,1,16,256]{3,2,1,0:T(8,128)(2,1)S(1)} %get-tuple-element.15), channel_id=1, source_target_pairs={{1,0},{3,2},{5,4},{7,6},{9,8},{11,10},{13,12},{15,14},{17,16},{19,... | collective-permute-start | bytes 24584 | tf_op jit(solution)/shard_map/ppermute | solution.py:24
  4.6 49.9 %collective-permute-start = (bf16[1,1,16,256]{3,2,1,0:T(8,128)(2,1)S(1)}, bf16[1,1,16,256]{3,2,1,0:T(8,128)(2,1)S(1)}, u32[]{:S(2)}, u32[]{:S(2)}) collective-permute-start(bf16[1,1,16,256]{3,2,1,0:T(8,128)(2,1)S(1)} %get-tuple-element.14), channel_id=1, source_target_pairs={{0,1},{2,3},{4,5},{6,7},{8,9},{10,11},{12,13},{14,15},{16,17},{18,... | collective-permute-start | bytes 24584 | tf_op jit(solution)/shard_map/ppermute | solution.py:21
  8.6 46.0 %copy-start.3 = (bf16[3,3,256,256]{3,2,1,0:T(8,128)(2,1)S(1)}, bf16[3,3,256,256]{3,2,1,0:T(8,128)(2,1)}, u32[]{:S(2)}) copy-start(bf16[3,3,256,256]{3,2,1,0:T(8,128)(2,1)} %param.18) | copy-start | bytes 3538948
  55.1 0.9 %copy-start.9 = (bf16[256,64]{0,1:T(8,128)(2,1)S(1)}, bf16[256,64]{0,1:T(8,128)(2,1)}, u32[]{:S(2)}) copy-start(bf16[256,64]{0,1:T(8,128)(2,1)} %param.19) | copy-start | bytes 98308
  55.8 19.4 %copy-start.1 = (bf16[64,256]{1,0:T(8,128)(2,1)S(1)}, bf16[64,256]{1,0:T(8,128)(2,1)}, u32[]{:S(2)}) copy-start(bf16[64,256]{1,0:T(8,128)(2,1)} %param.22) | copy-start | bytes 98308
  56.6 20.2 %copy-start.6 = (bf16[1,8,1024]{2,1,0:T(8,128)(2,1)}, bf16[1,8,1024]{2,1,0:T(8,128)(2,1)S(1)}, u32[]{:S(2)}) copy-start(bf16[1,8,1024]{2,1,0:T(8,128)(2,1)S(1)} %reshape.196) | copy-start | bytes 49156
  58.4 12.0 %collective-permute-start.2 = (bf16[1,16,1024]{2,1,0:T(8,128)(2,1)S(1)}, bf16[1,16,1024]{2,1,0:T(8,128)(2,1)S(1)}, u32[]{:S(2)}, u32[]{:S(2)}) collective-permute-start(bf16[1,16,1024]{2,1,0:T(8,128)(2,1)S(1)} %all_gather.6), channel_id=1, source_target_pairs={{0,2},{2,4},{4,6},{6,8},{8,10},{10,12},{12,14},{14,16},{16,18},{18... | collective-permute-start | bytes 98312 | tf_op jit(solution)/shard_map/ppermute | solution.py:13
  61.9 8.6 %collective-permute-start.3 = (bf16[1,16,1024]{2,1,0:T(8,128)(2,1)S(1)}, bf16[1,16,1024]{2,1,0:T(8,128)(2,1)S(1)}, u32[]{:S(2)}, u32[]{:S(2)}) collective-permute-start(bf16[1,16,1024]{2,1,0:T(8,128)(2,1)S(1)} %all_gather.6), channel_id=1, source_target_pairs={{0,4},{2,6},{4,8},{6,10},{8,12},{10,14},{12,16},{14,18},{16,20},{1... | collective-permute-start | bytes 98312 | tf_op jit(solution)/shard_map/ppermute | solution.py:13
  68.0 6.7 %collective-permute-start.4 = (bf16[1,16,1024]{2,1,0:T(8,128)(2,1)S(1)}, bf16[1,16,1024]{2,1,0:T(8,128)(2,1)S(1)}, u32[]{:S(2)}, u32[]{:S(2)}) collective-permute-start(bf16[1,16,1024]{2,1,0:T(8,128)(2,1)S(1)} %all_gather.6), channel_id=1, source_target_pairs={{0,6},{2,8},{4,10},{6,12},{8,14},{10,16},{12,18},{14,20},{16,22},{... | collective-permute-start | bytes 98312 | tf_op jit(solution)/shard_map/ppermute | solution.py:13
  77.0 0.9 %copy-start.5 = (bf16[256,256]{1,0:T(8,128)(2,1)S(1)}, bf16[256,256]{1,0:T(8,128)(2,1)}, u32[]{:S(2)}) copy-start(bf16[256,256]{1,0:T(8,128)(2,1)} %param.24) | copy-start | bytes 393220
where the time goes:
time: 79.8 us; the launch traced here: 78.9 us
  blocking collectives  36.9 us (46%)
  starting transfers between devices  15.7 us (20%)
  matrix products  12.9 us (16%)
  other arithmetic  4.59 us (6%)
  waiting for transfers between devices  4.19 us (5%)
  local copies, waits for them, and re-layouts  2.96 us (4%)
  between operations  1.72 us (2%)
    all_gather x1, blocking collectives, body(): all_pointers = lax.all_gather(pointers, 'tm', axis=0, tiled=True)  32.6 us
    ppermute x3, starting transfers between devices, from_behind(): return lax.ppermute(block, axis, route)  11.4 us
    ppermute x3, waiting for transfers between devices, from_behind(): return lax.ppermute(block, axis, route)  4.18 us
    ppermute x1, starting transfers between devices, with_halo(): lax.ppermute(lax.slice_in_dim(block, block.shape[dim] - width, None, axis...  3.03 us
    psum x1, blocking collectives, body(): pooled = lax.psum(partial_value, 'space')  2.45 us
    all_gather x1, blocking collectives, body(): carried = lax.all_gather(memory, 'space', axis=1, tiled=True)  1.83 us
  transfers between devices with their start and end apart: 5, of which 1 were waited for; matrix products, arithmetic and copies ran while one was open for 15% of the time, Pallas kernels for 0%

commit v1 on v0

--- a/solution.py
+++ b/solution.py
@@ -1,3 +1,4 @@
+import functools
 import jax
 import jax.numpy as jnp
 from jax import lax
@@ -5,6 +6,28 @@
 
 MEMS = 3
 POINTERS = 16
+
+
+def apply_ways(base_x, shard_axis):
+    seen_now = lax.axis_size(shard_axis)
+    r_now = lax.axis_index(shard_axis)
+    u1, z1, inter = (seen_now, r_now, base_x.shape[0])
+    local_next, y_new = (base_x, 1)
+    while y_new < u1:
+        local_next = jnp.concatenate(
+            [
+                local_next,
+                lax.ppermute(
+                    local_next, shard_axis, [(num, (num - y_new) % u1) for num in range(u1)]
+                ),
+            ],
+            axis=0,
+        )
+        y_new = 2 * y_new
+    return jnp.roll(local_next, z1 * inter, axis=0)
+
+
+layers_all_advance = functools.partial(apply_ways, shard_axis="tm")
 
 
 def from_behind(block, axis, distance):
@@ -107,7 +130,7 @@
         jnp.bfloat16
     )
     pointers = jnp.dot(normed, w_ptr, preferred_element_type=jnp.float32).astype(jnp.bfloat16)
-    all_pointers = lax.all_gather(pointers, "tm", axis=0, tiled=True)
+    all_pointers = layers_all_advance(pointers)
     hop_count = (MEMS + frames_dev - 1) // frames_dev
     carried = lax.all_gather(memory, "space", axis=1, tiled=True)
     history = jnp.concatenate(

time: 79.8 us -> 61 us (0.76)
  the two profiles are of different devices: /device:TPU:24 before, /device:TPU:0 now
where the time goes in v1:
time: 61 us; the launch traced here: 60.2 us
  starting transfers between devices  23.7 us (39%)
  matrix products  12.3 us (20%)
  waiting for transfers between devices  11.7 us (19%)
  other arithmetic  4.51 us (7%)
  blocking collectives  4.41 us (7%)
  local copies, waits for them, and re-layouts  1.83 us (3%)
  between operations  1.75 us (3%)
    ppermute x3, starting transfers between devices, from_behind(): return lax.ppermute(block, axis, route)  11.3 us
    ppermute x4, waiting for transfers between devices, apply_ways(): lax.ppermute(local_next, shard_axis, [(num, (num - y_new) % u1) for num i...  10.2 us
    ppermute x4, starting transfers between devices, apply_ways(): lax.ppermute(local_next, shard_axis, [(num, (num - y_new) % u1) for num i...  8.14 us
    ppermute x1, starting transfers between devices, with_halo(): lax.ppermute(lax.slice_in_dim(block, block.shape[dim] - width, None, axis...  3.03 us
    psum x1, blocking collectives, body(): pooled = lax.psum(partial_value, 'space')  2.58 us
    all_gather x1, blocking collectives, body(): carried = lax.all_gather(memory, 'space', axis=1, tiled=True)  1.83 us
    dot_general x4, matrix products, attend(): lax.dot_general(query, key_rows, (((1,), (1,)), ((), ())), preferred_elem...  1.45 us
    ppermute x3, waiting for transfers between devices, from_behind(): return lax.ppermute(block, axis, route)  1.44 us
  transfers between devices with their start and end apart: 9, of which 4 were waited for; matrix products, arithmetic and copies ran while one was open for 16% of the time, Pallas kernels for 0%

profile of v1, /device:TPU:0, one launch (start us, length us, event | category | flops | bytes accessed | tf_op | source)
XLA Modules:
  0.0 60.2 jit_solution(15603972470256879242)
XLA Ops:
  0.7 0.7 %convert_element_type.111 = f32[256]{0:T(256)S(1)} convert(bf16[256]{0:T(256)(128)(2,1)} %param.17) | non-fusion elementwise | flops 256 | bytes 1536 | tf_op jit(solution)/shard_map/convert_element_type | solution.py:104
  1.4 0.8 %convert_bitcast_fusion = (bf16[8,16,1]{1,0,2:T(8,128)(2,1)S(1)}, f32[1,8,16]{2,1,0:T(8,128)S(1)}) fusion(s32[1,8,16]{2,1,0:T(8,128)} %param.15), kind=kLoop, calls=%fused_computation.129 | loop fusion | flops 256 | bytes 1280 | tf_op jit(solution)/shard_map/reshape.131
  2.2 1.0 %fusion.12 = bf16[128,256]{1,0:T(8,128)(2,1)S(1)} fusion(bf16[128,256]{1,0:T(8,128)(2,1)} %bitcast.104, bf16[256,256]{1,0:T(8,128)(2,1)S(1)} %copy-done, f32[256]{0:T(256)S(1)} %convert_element_type.111, f32[128]{0:T(128)S(1)} %convert_element_type.110), kind=kOutput, calls=%fused_computation.29 | convolution fusion | flops 16875520 | bytes 263680 | tf_op jit(solution)/shard_map/dot_general | solution.py:103
  3.2 1.3 %collective-permute-start.1 = (bf16[1,1,16,256]{3,2,1,0:T(8,128)(2,1)S(1)}, bf16[1,1,16,256]{3,2,1,0:T(8,128)(2,1)S(1)}, u32[]{:S(2)}, u32[]{:S(2)}) collective-permute-start(bf16[1,1,16,256]{3,2,1,0:T(8,128)(2,1)S(1)} %get-tuple-element.15), channel_id=1, source_target_pairs={{1,0},{3,2},{5,4},{7,6},{9,8},{11,10},{13,12},{15,14},{17,16},{19,... | collective-permute-start | bytes 24584 | tf_op jit(solution)/shard_map/ppermute | solution.py:47
  4.5 3.0 %collective-permute-start = (bf16[1,1,16,256]{3,2,1,0:T(8,128)(2,1)S(1)}, bf16[1,1,16,256]{3,2,1,0:T(8,128)(2,1)S(1)}, u32[]{:S(2)}, u32[]{:S(2)}) collective-permute-start(bf16[1,1,16,256]{3,2,1,0:T(8,128)(2,1)S(1)} %get-tuple-element.14), channel_id=1, source_target_pairs={{0,1},{2,3},{4,5},{6,7},{8,9},{10,11},{12,13},{14,15},{16,17},{18,... | collective-permute-start | bytes 24584 | tf_op jit(solution)/shard_map/ppermute | solution.py:44
  7.6 1.0 %convolution_bitcast_fusion = f32[1,256]{1,0:T(1,128)S(1)} fusion(bf16[1,8,16,256]{3,2,1,0:T(8,128)(2,1)} %param.14, bf16[8,16,1]{1,0,2:T(8,128)(2,1)S(1)} %get-tuple-element.19), kind=kOutput, calls=%fused_computation.36 | convolution fusion | flops 65536 | bytes 66816 | tf_op jit(solution)/shard_map/ft,ftd->fd/dot_general | solution.py:122
  8.6 2.6 %psum.7 = f32[1,256]{1,0:T(1,128)S(1)} all-reduce(f32[1,256]{1,0:T(1,128)S(1)} %convolution_bitcast_fusion), channel_id=1, replica_groups=mesh['tm'=16,'space'=2] {'space'}, use_global_device_ids=true, to_apply=%region_5.6 | all-reduce | flops 256 | bytes 2048 | tf_op jit(solution)/shard_map/psum | solution.py:128
  12.5 1.0 %fusion.94 = f32[1,256]{1,0:T(1,128)S(1)} fusion(bf16[256,256]{1,0:T(8,128)(2,1)} %param.20, f32[1,256]{1,0:T(1,128)S(1)} %psum.7, f32[]{:T(128)S(6)} %rsqrt.17), kind=kOutput, calls=%fused_computation.133 | convolution fusion | flops 131584 | bytes 133124 | tf_op jit(solution)/shard_map/dot_general | solution.py:132
  13.6 7.0 %collective-permute-start.5 = (bf16[1,256]{1,0:T(2,128)(2,1)S(1)}, bf16[1,256]{1,0:T(2,128)(2,1)S(1)}, u32[]{:S(2)}, u32[]{:S(2)}) collective-permute-start(bf16[1,256]{1,0:T(2,128)(2,1)S(1)} %convert_element_type.121), channel_id=1, source_target_pairs={{0,30},{2,0},{4,2},{6,4},{8,6},{10,8},{12,10},{14,12},{16,14},{18,... | collective-permute-start | bytes 1544 | tf_op jit(solution)/shard_map/ppermute | solution.py:20
  20.6 0.9 %convert_reduce_fusion = f32[8,16]{1,0:T(8,128)S(1)} fusion(bf16[1,8,16,256]{3,2,1,0:T(8,128)(2,1)} %param.14), kind=kLoop, calls=%fused_computation.42 | loop fusion | flops 65408 | bytes 66048 | tf_op jit(solution)/shard_map/reduce_sum | solution.py:166
  21.5 1.0 %fusion.22 = f32[8,16]{1,0:T(8,128)S(1)} fusion(bf16[1,8,16,256]{3,2,1,0:T(8,128)(2,1)} %param.14, f32[8,16]{1,0:T(8,128)S(1)} %broadcast_multiply_fusion), kind=kLoop, calls=%fused_computation.50 | loop fusion | flops 130944 | bytes 66560 | tf_op jit(solution)/shard_map/reduce_sum | solution.py:168
  22.7 0.9 %fusion.117 = f32[3,256]{1,0:T(4,128)S(1)} fusion(bf16[3,64]{1,0:T(4,128)(2,1)} %param.25, bf16[64,256]{1,0:T(8,128)(2,1)} %param.22), kind=kOutput, calls=%fused_computation.160 | convolution fusion | flops 98304 | bytes 36224 | tf_op jit(solution)/shard_map/dot_general | solution.py:146
  23.6 0.9 %fusion.100 = f32[1,256]{1,0:T(1,128)S(1)} fusion(bf16[64,256]{1,0:T(8,128)(2,1)} %param.22, bf16[64]{0:T(256)(128)(2,1)} %param.27), kind=kOutput, calls=%fused_computation.140 | convolution fusion | flops 32768 | bytes 33920 | tf_op jit(solution)/shard_map/dot_general | solution.py:152
  24.5 1.2 %fusion.11 = bf16[128,256]{1,0:T(8,128)(2,1)S(1)} fusion(bf16[256,256]{1,0:T(8,128)(2,1)} %param.21, bf16[128,256]{1,0:T(8,128)(2,1)} %bitcast.105, f32[128]{0:T(128)S(1)} %rsqrt.16, f32[128]{0:T(128)S(1)} %div.40), kind=kOutput, calls=%fused_computation.28 | convolution fusion | flops 16973824 | bytes 263168 | tf_op jit(solution)/shard_map/dot_general | solution.py:171
  25.7 0.9 %fusion.98 = f32[1,256]{1,0:T(1,128)S(1)} fusion(bf16[64,256]{1,0:T(8,128)(2,1)} %param.23, bf16[64]{0:T(256)(128)(2,1)} %param.27), kind=kOutput, calls=%fused_computation.138 | convolution fusion | flops 32768 | bytes 33920 | tf_op jit(solution)/shard_map/dot_general | solution.py:155
  27.2 3.1 %collective-permute-done.6 = bf16[2,256]{1,0:T(2,128)(2,1)S(1)} collective-permute-done((bf16[2,256]{1,0:T(2,128)(2,1)S(1)}, bf16[2,256]{1,0:T(2,128)(2,1)S(1)}, u32[]{:S(2)}, u32[]{:S(2)}) %collective-permute-start.6) | collective-permute-done | bytes 1056 | tf_op jit(solution)/shard_map/ppermute | solution.py:20
  30.9 3.0 %collective-permute-done.7 = bf16[4,256]{1,0:T(4,128)(2,1)S(1)} collective-permute-done((bf16[4,256]{1,0:T(4,128)(2,1)S(1)}, bf16[4,256]{1,0:T(4,128)(2,1)S(1)}, u32[]{:S(2)}, u32[]{:S(2)}) %collective-permute-start.7) | collective-permute-done | bytes 2080 | tf_op jit(solution)/shard_map/ppermute | solution.py:20
  34.2 4.2 %collective-permute-done.8 = bf16[8,256]{1,0:T(8,128)(2,1)S(1)} collective-permute-done((bf16[8,256]{1,0:T(8,128)(2,1)S(1)}, bf16[8,256]{1,0:T(8,128)(2,1)S(1)}, u32[]{:S(2)}, u32[]{:S(2)}) %collective-permute-start.8) | collective-permute-done | bytes 4128 | tf_op jit(solution)/shard_map/ppermute | solution.py:20
  41.2 1.8 %all_gather.3 = bf16[1,16,1024]{2,1,0:T(8,128)(2,1)S(1)} all-gather(bf16[1,8,1024]{2,1,0:T(8,128)(2,1)S(1)} %reshape.196), channel_id=1, replica_groups=mesh['tm'=16,'space'=2] {'space'}, dimensions={1}, use_global_device_ids=true | all-gather | bytes 49152 | tf_op jit(solution)/shard_map/all_gather | solution.py:135
  43.0 1.3 %collective-permute-start.2 = (bf16[1,16,1024]{2,1,0:T(8,128)(2,1)S(1)}, bf16[1,16,1024]{2,1,0:T(8,128)(2,1)S(1)}, u32[]{:S(2)}, u32[]{:S(2)}) collective-permute-start(bf16[1,16,1024]{2,1,0:T(8,128)(2,1)S(1)} %all_gather.3), channel_id=1, source_target_pairs={{0,2},{2,4},{4,6},{6,8},{8,10},{10,12},{12,14},{14,16},{16,18},{18... | collective-permute-start | bytes 98312 | tf_op jit(solution)/shard_map/ppermute | solution.py:36
  44.4 5.2 %collective-permute-start.3 = (bf16[1,16,1024]{2,1,0:T(8,128)(2,1)S(1)}, bf16[1,16,1024]{2,1,0:T(8,128)(2,1)S(1)}, u32[]{:S(2)}, u32[]{:S(2)}) collective-permute-start(bf16[1,16,1024]{2,1,0:T(8,128)(2,1)S(1)} %all_gather.3), channel_id=1, source_target_pairs={{0,4},{2,6},{4,8},{6,10},{8,12},{10,14},{12,16},{14,18},{16,20},{1... | collective-permute-start | bytes 98312 | tf_op jit(solution)/shard_map/ppermute | solution.py:36
  49.6 4.8 %collective-permute-start.4 = (bf16[1,16,1024]{2,1,0:T(8,128)(2,1)S(1)}, bf16[1,16,1024]{2,1,0:T(8,128)(2,1)S(1)}, u32[]{:S(2)}, u32[]{:S(2)}) collective-permute-start(bf16[1,16,1024]{2,1,0:T(8,128)(2,1)S(1)} %all_gather.3), channel_id=1, source_target_pairs={{0,6},{2,8},{4,10},{6,12},{8,14},{10,16},{12,18},{14,20},{16,22},{... | collective-permute-start | bytes 98312 | tf_op jit(solution)/shard_map/ppermute | solution.py:36
  54.5 1.4 %collective-permute-done.4 = bf16[1,16,1024]{2,1,0:T(8,128)(2,1)S(1)} collective-permute-done((bf16[1,16,1024]{2,1,0:T(8,128)(2,1)S(1)}, bf16[1,16,1024]{2,1,0:T(8,128)(2,1)S(1)}, u32[]{:S(2)}, u32[]{:S(2)}) %collective-permute-start.4) | collective-permute-done | bytes 32800 | tf_op jit(solution)/shard_map/ppermute | solution.py:36
  59.3 1.0 %fusion.13 = bf16[128,256]{1,0:T(8,128)(2,1)} fusion(bf16[256,256]{1,0:T(8,128)(2,1)S(1)} %copy-done.5, f32[128,256]{1,0:T(8,128)S(1)} %convolution_add_fusion.5, bf16[128,256]{1,0:T(8,128)(2,1)S(1)} %bitcast.106, bf16[1,256]{1,0:T(2,128)(2,1)S(1)} %convert_element_type.132, bf16[64,256]{1,0:T(8,128)(2,1)S(1)} %convolution_convert_fusion.1, ...), kind=kOutput, calls=%fused_computation.30 | convolution fusion | flops 21292416 | bytes 460800 | tf_op jit(solution)/shard_map/dot_general | solution.py:199
  (89 shorter events, 8.5 us)
Async XLA Ops:
  0.6 1.6 %copy-start = (bf16[256,256]{1,0:T(8,128)(2,1)S(1)}, bf16[256,256]{1,0:T(8,128)(2,1)}, u32[]{:S(2)}) copy-start(bf16[256,256]{1,0:T(8,128)(2,1)} %param.16) | copy-start | bytes 393220
  0.6 38.0 %copy-start.1 = (bf16[64,256]{1,0:T(8,128)(2,1)S(1)}, bf16[64,256]{1,0:T(8,128)(2,1)}, u32[]{:S(2)}) copy-start(bf16[64,256]{1,0:T(8,128)(2,1)} %param.22) | copy-start | bytes 98308
  0.7 33.4 %copy-start.8 = (bf16[16,256]{1,0:T(8,128)(2,1)S(1)}, bf16[16,256]{1,0:T(8,128)(2,1)}, u32[]{:S(2)}) copy-start(bf16[16,256]{1,0:T(8,128)(2,1)} %param.26) | copy-start | bytes 24580
  3.2 35.8 %collective-permute-start.1 = (bf16[1,1,16,256]{3,2,1,0:T(8,128)(2,1)S(1)}, bf16[1,1,16,256]{3,2,1,0:T(8,128)(2,1)S(1)}, u32[]{:S(2)}, u32[]{:S(2)}) collective-permute-start(bf16[1,1,16,256]{3,2,1,0:T(8,128)(2,1)S(1)} %get-tuple-element.15), channel_id=1, source_target_pairs={{1,0},{3,2},{5,4},{7,6},{9,8},{11,10},{13,12},{15,14},{17,16},{19,... | collective-permute-start | bytes 24584 | tf_op jit(solution)/shard_map/ppermute | solution.py:47
  4.5 34.5 %collective-permute-start = (bf16[1,1,16,256]{3,2,1,0:T(8,128)(2,1)S(1)}, bf16[1,1,16,256]{3,2,1,0:T(8,128)(2,1)S(1)}, u32[]{:S(2)}, u32[]{:S(2)}) collective-permute-start(bf16[1,1,16,256]{3,2,1,0:T(8,128)(2,1)S(1)} %get-tuple-element.14), channel_id=1, source_target_pairs={{0,1},{2,3},{4,5},{6,7},{8,9},{10,11},{12,13},{14,15},{16,17},{18,... | collective-permute-start | bytes 24584 | tf_op jit(solution)/shard_map/ppermute | solution.py:44
  8.6 30.6 %copy-start.3 = (bf16[3,3,256,256]{3,2,1,0:T(8,128)(2,1)S(1)}, bf16[3,3,256,256]{3,2,1,0:T(8,128)(2,1)}, u32[]{:S(2)}) copy-start(bf16[3,3,256,256]{3,2,1,0:T(8,128)(2,1)} %param.18) | copy-start | bytes 3538948
  13.6 25.8 %copy-start.7 = (bf16[1,256]{1,0:T(2,128)(2,1)}, bf16[1,256]{1,0:T(2,128)(2,1)S(1)}, u32[]{:S(2)}) copy-start(bf16[1,256]{1,0:T(2,128)(2,1)S(1)} %convert_element_type.121) | copy-start | bytes 1540
  13.6 13.0 %collective-permute-start.5 = (bf16[1,256]{1,0:T(2,128)(2,1)S(1)}, bf16[1,256]{1,0:T(2,128)(2,1)S(1)}, u32[]{:S(2)}, u32[]{:S(2)}) collective-permute-start(bf16[1,256]{1,0:T(2,128)(2,1)S(1)} %convert_element_type.121), channel_id=1, source_target_pairs={{0,30},{2,0},{4,2},{6,4},{8,6},{10,8},{12,10},{14,12},{16,14},{18,... | collective-permute-start | bytes 1544 | tf_op jit(solution)/shard_map/ppermute | solution.py:20
  26.6 3.6 %collective-permute-start.6 = (bf16[2,256]{1,0:T(2,128)(2,1)S(1)}, bf16[2,256]{1,0:T(2,128)(2,1)S(1)}, u32[]{:S(2)}, u32[]{:S(2)}) collective-permute-start(bf16[2,256]{1,0:T(2,128)(2,1)S(1)} %pad_maximum_fusion.5), channel_id=1, source_target_pairs={{0,28},{2,30},{4,0},{6,2},{8,4},{10,6},{12,8},{14,10},{16,12},{18,... | collective-permute-start | bytes 3080 | tf_op jit(solution)/shard_map/ppermute | solution.py:20
  30.2 3.6 %collective-permute-start.7 = (bf16[4,256]{1,0:T(4,128)(2,1)S(1)}, bf16[4,256]{1,0:T(4,128)(2,1)S(1)}, u32[]{:S(2)}, u32[]{:S(2)}) collective-permute-start(bf16[4,256]{1,0:T(4,128)(2,1)S(1)} %pad_maximum_fusion.4), channel_id=1, source_target_pairs={{0,24},{2,26},{4,28},{6,30},{8,0},{10,2},{12,4},{14,6},{16,8},{18,... | collective-permute-start | bytes 6152 | tf_op jit(solution)/shard_map/ppermute | solution.py:20
  33.9 4.6 %collective-permute-start.8 = (bf16[8,256]{1,0:T(8,128)(2,1)S(1)}, bf16[8,256]{1,0:T(8,128)(2,1)S(1)}, u32[]{:S(2)}, u32[]{:S(2)}) collective-permute-start(bf16[8,256]{1,0:T(8,128)(2,1)S(1)} %pad_maximum_fusion.3), channel_id=1, source_target_pairs={{0,16},{2,18},{4,20},{6,22},{8,24},{10,26},{12,28},{14,30},{16,0},... | collective-permute-start | bytes 12296 | tf_op jit(solution)/shard_map/ppermute | solution.py:20
  39.7 0.9 %copy-start.9 = (bf16[256,64]{0,1:T(8,128)(2,1)S(1)}, bf16[256,64]{0,1:T(8,128)(2,1)}, u32[]{:S(2)}) copy-start(bf16[256,64]{0,1:T(8,128)(2,1)} %param.19) | copy-start | bytes 98308
  39.9 14.4 %copy-start.4 = (bf16[64,256]{1,0:T(8,128)(2,1)S(1)}, bf16[64,256]{1,0:T(8,128)(2,1)}, u32[]{:S(2)}) copy-start(bf16[64,256]{1,0:T(8,128)(2,1)} %param.23) | copy-start | bytes 98308
  41.2 16.8 %copy-start.6 = (bf16[1,8,1024]{2,1,0:T(8,128)(2,1)}, bf16[1,8,1024]{2,1,0:T(8,128)(2,1)S(1)}, u32[]{:S(2)}) copy-start(bf16[1,8,1024]{2,1,0:T(8,128)(2,1)S(1)} %reshape.196) | copy-start | bytes 49156
  43.0 11.4 %collective-permute-start.2 = (bf16[1,16,1024]{2,1,0:T(8,128)(2,1)S(1)}, bf16[1,16,1024]{2,1,0:T(8,128)(2,1)S(1)}, u32[]{:S(2)}, u32[]{:S(2)}) collective-permute-start(bf16[1,16,1024]{2,1,0:T(8,128)(2,1)S(1)} %all_gather.3), channel_id=1, source_target_pairs={{0,2},{2,4},{4,6},{6,8},{8,10},{10,12},{12,14},{14,16},{16,18},{18... | collective-permute-start | bytes 98312 | tf_op jit(solution)/shard_map/ppermute | solution.py:36
  44.4 10.1 %collective-permute-start.3 = (bf16[1,16,1024]{2,1,0:T(8,128)(2,1)S(1)}, bf16[1,16,1024]{2,1,0:T(8,128)(2,1)S(1)}, u32[]{:S(2)}, u32[]{:S(2)}) collective-permute-start(bf16[1,16,1024]{2,1,0:T(8,128)(2,1)S(1)} %all_gather.3), channel_id=1, source_target_pairs={{0,4},{2,6},{4,8},{6,10},{8,12},{10,14},{12,16},{14,18},{16,20},{1... | collective-permute-start | bytes 98312 | tf_op jit(solution)/shard_map/ppermute | solution.py:36
  49.6 6.3 %collective-permute-start.4 = (bf16[1,16,1024]{2,1,0:T(8,128)(2,1)S(1)}, bf16[1,16,1024]{2,1,0:T(8,128)(2,1)S(1)}, u32[]{:S(2)}, u32[]{:S(2)}) collective-permute-start(bf16[1,16,1024]{2,1,0:T(8,128)(2,1)S(1)} %all_gather.3), channel_id=1, source_target_pairs={{0,6},{2,8},{4,10},{6,12},{8,14},{10,16},{12,18},{14,20},{16,22},{... | collective-permute-start | bytes 98312 | tf_op jit(solution)/shard_map/ppermute | solution.py:36
  58.3 0.8 %copy-start.2 = (bf16[1,8,16,256]{3,2,1,0:T(8,128)(2,1)S(1)}, bf16[1,8,16,256]{3,2,1,0:T(8,128)(2,1)}, u32[]{:S(2)}) copy-start(bf16[1,8,16,256]{3,2,1,0:T(8,128)(2,1)} %param.14) | copy-start | bytes 196612
  58.3 0.9 %copy-start.5 = (bf16[256,256]{1,0:T(8,128)(2,1)S(1)}, bf16[256,256]{1,0:T(8,128)(2,1)}, u32[]{:S(2)}) copy-start(bf16[256,256]{1,0:T(8,128)(2,1)} %param.24) | copy-start | bytes 393220
